TPU v7x, 256 devices: a whole 4x4x8 slice. The times are simulated.
256 devices in a mesh: coarse: 8 (over x, core), fine: 32 (over z, y).
Axes of the slice: x: 4, y: 4, z: 8, core: 2. Of those that a mesh axis runs over, the one named last changes fastest.
Arguments:
- tokens: bfloat16 [131072, 1024], P(('coarse', 'fine'))
- w_qkv: bfloat16 [1024, 3072], replicated, may hold values from -0.1875 to 0.1875
- w_coarse_out: bfloat16 [1024, 1024], replicated, may hold values from -0.1875 to 0.1875
- w_kv2: bfloat16 [1024, 2048], replicated, may hold values from -0.1875 to 0.1875
- w_out: bfloat16 [1024, 1024], replicated, may hold values from -0.1875 to 0.1875
- seg_start: int32 [4096], P('coarse'), may hold values from 0 to 131071, as said below
- seg_end: int32 [4096], P('coarse'), may hold values from 1 to 131072, as said below
- block_lists: int32 [512, 8], P(('coarse', 'fine')), may hold values from 0 to 255, as said below
Outputs:
- mixed: bfloat16 [131072, 1024], P(('coarse', 'fine'))
Inputs may be any that keep to these rules, and one draw needn't show every extreme that they name: `seg_start`: for each coarse owner c, the segments c*512 to (c+1)*512 - 1 are nonempty and pairwise disjoint and lie within time steps c*16384 to (c+1)*16384 - 1, listed in an order that does not follow time; steps outside all segments belong to none; segment lengths are uneven. seg_end[s] > seg_start[s]. `block_lists`: row n names 8 distinct coarse key blocks (block b holds segments b*16 to (b+1)*16 - 1), all among the blocks of owners c-1, c and c+1 taken cyclically over the owners, where c = n*256 // 16384 is the owner of the row's time steps.
All inputs are finite; a program needn't handle non-finite values.
Results may differ from a plain program's by a relative error of at most 0.017.
Values may be sent and summed in bfloat16 or wider, within the bound.
A program may use at most 128 MiB of HBM per device.

v0:
```python
import math
import jax
import jax.numpy as jnp
from jax import lax
from jax.sharding import PartitionSpec as P

HEADS = 8
KB = 16
QB = 256


def padded(cells, sides, width):
    for axis, dim in sides:
        count = lax.axis_size(axis)
        head = lax.slice_in_dim(cells, 0, width, axis=dim)
        tail = lax.slice_in_dim(cells, cells.shape[dim] - width, cells.shape[dim], axis=dim)
        cells = jnp.concatenate(
            [
                lax.ppermute(tail, axis, [(i, (i + 1) % count) for i in range(count)]),
                cells,
                lax.ppermute(head, axis, [((i + 1) % count, i) for i in range(count)]),
            ],
            axis=dim,
        )
    return cells


def attend_heads(queries, keys, content_elements, allowed):
    count = queries.shape[0]
    head_size = queries.shape[1] // HEADS
    query_heads = queries.reshape(count, HEADS, head_size)
    key_heads = keys.reshape(keys.shape[0], HEADS, head_size)
    value_heads = content_elements.reshape(content_elements.shape[0], HEADS, head_size)
    scores = jnp.einsum("qhd,khd->hqk", query_heads, key_heads, preferred_element_type=jnp.float32)
    scores = scores * (1.0 / math.sqrt(head_size))
    scores = jnp.where(allowed[None], scores, -1e30)
    highest = jnp.max(scores, axis=-1, keepdims=True)
    expos = jnp.exp(scores - highest)
    weights = (expos / jnp.sum(expos, axis=-1, keepdims=True)).astype(jnp.bfloat16)
    blended = jnp.einsum("hqk,khd->qhd", weights, value_heads, preferred_element_type=jnp.float32)
    return blended.astype(jnp.bfloat16).reshape(count, HEADS * head_size)


def normalize(content_elements):
    return content_elements * lax.rsqrt(
        jnp.mean(content_elements * content_elements, axis=-1, keepdims=True) + 1e-06
    )


def body(tokens, w_qkv, w_coarse_out, w_kv2, w_out, seg_start, seg_end, block_lists):
    rows_here = tokens.shape[0]
    width = tokens.shape[1]
    fine_count = lax.axis_size("fine")
    coarse_count = lax.axis_size("coarse")
    fine_index = lax.axis_index("fine")
    coarse_index = lax.axis_index("coarse")
    seg_owned = seg_start.shape[0]
    first_row = coarse_index * (rows_here * fine_count) + fine_index * rows_here
    positions = first_row + jnp.arange(rows_here, dtype=jnp.int32)
    member = (
        (positions[None, :] >= seg_start[:, None]) & (positions[None, :] < seg_end[:, None])
    ).astype(jnp.bfloat16)
    sums = lax.psum_scatter(
        jnp.dot(member, tokens, preferred_element_type=jnp.float32).astype(jnp.bfloat16),
        "fine",
        scatter_dimension=0,
        tiled=True,
    ).astype(jnp.float32)
    share_start = fine_index * KB
    spans = (
        lax.dynamic_slice_in_dim(seg_end, share_start, KB, 0)
        - lax.dynamic_slice_in_dim(seg_start, share_start, KB, 0)
    ).astype(jnp.float32)
    pooled = (sums / jnp.sqrt(spans)[:, None]).astype(jnp.bfloat16)
    coarse_proj = jnp.dot(pooled, w_qkv, preferred_element_type=jnp.float32)
    coarse_query = coarse_proj[:, :width].astype(jnp.bfloat16)
    coarse_pair = coarse_proj[:, width:].astype(jnp.bfloat16)
    owner_pairs = lax.all_gather(coarse_pair, "fine", axis=0, tiled=True)
    reach = seg_owned // 2
    window_table = padded(owner_pairs, (("coarse", 0),), reach)
    query_place = reach + share_start + jnp.arange(KB, dtype=jnp.int32)
    key_place = jnp.arange(window_table.shape[0], dtype=jnp.int32)
    allowed = jnp.abs(query_place[:, None] - key_place[None, :]) <= reach
    coarse_mix = attend_heads(
        coarse_query, window_table[:, :width], window_table[:, width:], allowed
    )
    context = jnp.dot(coarse_mix, w_coarse_out, preferred_element_type=jnp.float32)
    state = normalize(context).astype(jnp.bfloat16)
    payload = jnp.dot(state, w_kv2, preferred_element_type=jnp.float32).astype(jnp.bfloat16)
    seg_total = seg_owned * coarse_count
    owner_rows = lax.all_gather(payload, "fine", axis=0, tiled=True)
    second_table = padded(owner_rows, (("coarse", 0),), seg_owned)
    table_base = (coarse_index - 1) * seg_owned
    proj = jnp.dot(tokens, w_qkv, preferred_element_type=jnp.float32)
    query = proj[:, :width].astype(jnp.bfloat16)
    key_rows = proj[:, width : 2 * width].astype(jnp.bfloat16)
    value_rows = proj[:, 2 * width :].astype(jnp.bfloat16)
    listed_rows = (
        block_lists[:, :, None] * KB + jnp.arange(KB, dtype=jnp.int32)[None, None, :]
    ).reshape(block_lists.shape[0], -1)
    table_rows = jnp.mod(listed_rows - table_base, seg_total)
    block_rows = min(512, rows_here)
    sub_blocks = block_rows // QB
    remote_per_sub = table_rows.shape[1]
    query_group = jnp.arange(block_rows, dtype=jnp.int32) // QB
    remote_group = jnp.arange(sub_blocks * remote_per_sub, dtype=jnp.int32) // remote_per_sub
    allowed_fine = jnp.concatenate(
        [
            jnp.ones((block_rows, rows_here), dtype=bool),
            query_group[:, None] == remote_group[None, :],
        ],
        axis=1,
    )

    def query_block(number):
        wanted = table_rows.reshape(-1)
        remote = jnp.take(second_table, wanted, axis=0)
        keys = jnp.concatenate([key_rows, remote[:, :width]], axis=0)
        content_elements = jnp.concatenate([value_rows, remote[:, width:]], axis=0)
        return attend_heads(query, keys, content_elements, allowed_fine)

    attended = lax.map(query_block, jnp.arange(rows_here // block_rows, dtype=jnp.int32)).reshape(
        rows_here, width
    )
    projected = jnp.dot(attended, w_out, preferred_element_type=jnp.float32)
    return normalize(projected).astype(jnp.bfloat16)


def solution(mesh):
    placed = (
        P(("coarse", "fine"), None),
        P(),
        P(),
        P(),
        P(),
        P("coarse"),
        P("coarse"),
        P(("coarse", "fine"), None),
    )
    return jax.shard_map(
        body, mesh=mesh, in_specs=placed, out_specs=P(("coarse", "fine"), None), check_vma=False
    )
```

profile of v0, /device:TPU:1, one launch (start us, length us, event | category | flops | bytes accessed | tf_op | source)
XLA Modules:
  0.0 506.6 jit_solution(6676271423048525589)
XLA Ops:
  6.5 3.1 convolution_convert_fusion.3
  9.7 0.0 reduce-scatter.2.cloned.1.call-update
  9.7 0.0 all-gather.3.cloned.1.call-start
  9.8 0.8 convert_sqrt_fusion
  10.5 215.7 %reduce-scatter.2.cloned.1.call-done = bf16[16,1024]{1,0:T(8,128)(2,1)} async-done(((bf16[512,1024]{1,0:T(8,128)(2,1)}), bf16[16,1024]{1,0:T(8,128)(2,1)}) %reduce-scatter.2.cloned.1.call-update) | async-done | bytes 32784 | tf_op jit(solution)/shard_map/reduce_scatter | solution.py:63
  226.3 3.8 convolution_convert_fusion.1
  230.0 0.6 slice.55
  230.7 0.0 all-gather.3.cloned.1.call-update
  230.7 0.0 all-gather.5.cloned.1.call-start
  230.7 77.0 %all-gather.3.cloned.1.call-done = bf16[512,2048]{1,0:T(8,128)(2,1)} async-done(((bf16[16,2048]{1,0:T(8,128)(2,1)}), bf16[512,2048]{1,0:T(8,128)(2,1)}) %all-gather.3.cloned.1.call-update) | async-done | bytes 2097168 | tf_op jit(solution)/shard_map/all_gather | solution.py:78
  307.7 3.1 fusion.55
  310.8 6.5 %collective-permute-start = (bf16[256,2048]{1,0:T(8,128)(2,1)}, bf16[256,2048]{1,0:T(8,128)(2,1)}, u32[]{:S(2)}, u32[]{:S(2)}) collective-permute-start(bf16[256,2048]{1,0:T(8,128)(2,1)} %get-tuple-element.34), channel_id=1, source_target_pairs={{0,32},{32,64},{64,96},{96,128},{128,160},{160,192},{192,224},{224... | collective-permute-start | bytes 3145736 | tf_op jit(solution)/shard_map/ppermute | solution.py:19
  317.4 0.1 abs_compare_fusion
  317.5 12.0 %collective-permute-done = bf16[256,2048]{1,0:T(8,128)(2,1)} collective-permute-done((bf16[256,2048]{1,0:T(8,128)(2,1)}, bf16[256,2048]{1,0:T(8,128)(2,1)}, u32[]{:S(2)}, u32[]{:S(2)}) %collective-permute-start) | collective-permute-done | bytes 1048608 | tf_op jit(solution)/shard_map/ppermute | solution.py:19
  329.4 1.3 constant_dynamic-update-slice_fusion.2
  330.8 0.1 constant_dynamic-update-slice_fusion.1
  330.9 0.9 collective-permute-done.1
  331.8 0.1 constant_dynamic-update-slice_fusion
  331.9 2.9 slice_bitcast_fusion.1
  334.8 2.4 fusion.57
  337.2 2.4 fusion.28
  339.6 2.1 multiply_reduce_fusion.1
  341.7 1.3 convolution_convert_fusion.2
  343.0 0.0 all-gather.5.cloned.1.call-update
  343.1 0.1 add.149
  343.2 0.1 add.167
  343.2 0.1 add.150
  343.3 0.1 add.152
  343.4 70.0 %all-gather.5.cloned.1.call-done = bf16[512,2048]{1,0:T(8,128)(2,1)} async-done(((bf16[16,2048]{1,0:T(8,128)(2,1)}), bf16[512,2048]{1,0:T(8,128)(2,1)}) %all-gather.5.cloned.1.call-update) | async-done | bytes 2097168 | tf_op jit(solution)/shard_map/all_gather | solution.py:91
  413.4 5.5 %collective-permute-start.3 = (bf16[512,2048]{1,0:T(8,128)(2,1)}, bf16[512,2048]{1,0:T(8,128)(2,1)S(1)}, u32[]{:S(2)}, u32[]{:S(2)}) collective-permute-start(bf16[512,2048]{1,0:T(8,128)(2,1)} %all-gather.5.cloned.1.call-done), channel_id=1, source_target_pairs={{32,0},{64,32},{96,64},{128,96},{160,128},{192,160},{224,192},{0,2... | collective-permute-start | bytes 6291464 | tf_op jit(solution)/shard_map/ppermute | solution.py:21
  418.9 1.1 collective-permute-start.2
  420.0 0.1 broadcast_compare_fusion
  420.2 0.1 concatenate.20
  420.3 6.5 %convolution_convert_fusion = bf16[512,3072]{1,0:T(8,128)(2,1)S(1)} fusion(bf16[512,1024]{1,0:T(8,128)(2,1)} %param.8, bf16[1024,3072]{1,0:T(8,128)(2,1)} %param.9), kind=kOutput, calls=%fused_computation.12 | convolution fusion | flops 3222798336 | bytes 10485760 | tf_op jit(solution)/shard_map/dot_general | solution.py:94
  426.9 1.8 slice_bitcast_fusion.2
  428.6 15.6 %collective-permute-done.3 = bf16[512,2048]{1,0:T(8,128)(2,1)S(1)} collective-permute-done((bf16[512,2048]{1,0:T(8,128)(2,1)}, bf16[512,2048]{1,0:T(8,128)(2,1)S(1)}, u32[]{:S(2)}, u32[]{:S(2)}) %collective-permute-start.3) | collective-permute-done | bytes 2097184 | tf_op jit(solution)/shard_map/ppermute | solution.py:21
  444.2 11.2 %pad_maximum_fusion = bf16[1536,2048]{1,0:T(8,128)(2,1)} fusion(bf16[512,2048]{1,0:T(8,128)(2,1)S(1)} %collective-permute-done.3, bf16[512,2048]{1,0:T(8,128)(2,1)S(1)} %copy-done.5, bf16[512,2048]{1,0:T(8,128)(2,1)S(1)} %collective-permute-done.2), kind=kLoop, calls=%fused_computation.7 | loop fusion | flops 18874368 | bytes 12582912 | tf_op jit(solution)/shard_map/concatenate | solution.py:17
  455.4 6.0 %gather_fusion = bf16[256,2048]{1,0:T(8,128)(2,1)S(1)} fusion(bf16[1536,2048]{1,0:T(8,128)(2,1)} %pad_maximum_fusion, s32[1024]{0:T(1024)S(1)} %pad_clamp_fusion), kind=kCustom, calls=%fused_computation | custom fusion | bytes 2098176 | tf_op jit(solution)/shard_map/while/body/eval_jaxpr/jit(_take)/gather | solution.py:117
  461.4 0.2 broadcast_select_fusion
  461.6 0.9 fusion.56
  462.4 0.3 copy-done.3
  462.7 1.3 pad_maximum_fusion.1
  464.0 2.6 copy.22
  466.6 7.7 %fusion.13 = f32[8,512,768]{2,1,0:T(8,128)} fusion(bf16[64,8,8,128]{3,2,1,0:T(8,128)(2,1)S(1)} %copy-done.4, bf16[256,1024]{1,0:T(8,128)(2,1)} %get-tuple-element.36, bf16[512,1024]{1,0:T(8,128)(2,1)} %get-tuple-element.22), kind=kOutput, calls=%fused_computation.25 | convolution fusion | flops 808452096 | bytes 15204352 | tf_op jit(solution)/shard_map/while/body/eval_jaxpr/qhd,khd->hqk/dot_general | solution.py:34
  474.3 16.3 %fusion.58 = (f32[8,512]{1,0:T(8,128)S(1)}, f32[8,512,768]{2,1,0:T(8,128)}) fusion(f32[8,512,768]{2,1,0:T(8,128)} %fusion.13, pred[512,768]{1,0:T(8,128)(4,1)S(1)} %concatenate.20), kind=kOutput, calls=%fused_computation.102 | output fusion | flops 18875136 | bytes 25575424 | tf_op jit(solution)/shard_map/while/body/eval_jaxpr/sub | solution.py:38
  490.7 6.9 %fusion.16 = bf16[8,128,512]{2,1,0:T(8,128)(2,1)S(1)} fusion(bf16[768,8,128]{0,2,1:T(8,128)(2,1)S(1)} %bitcast.73, f32[8,512,768]{2,1,0:T(8,128)} %get-tuple-element.43, f32[8,512]{1,0:T(8,128)S(1)} %get-tuple-element.42), kind=kOutput, calls=%fused_computation.31 | convolution fusion | flops 812122112 | bytes 15220736 | tf_op jit(solution)/shard_map/while/body/eval_jaxpr/hqk,khd->qhd/dot_general | solution.py:40
  497.5 1.4 multiply_reduce_fusion
  498.9 1.2 multiply_convert_fusion
  (30 shorter events, 0.1 us)
Async XLA Ops:
  6.5 491.0 %copy-start = (bf16[1024,1024]{1,0:T(8,128)(2,1)S(1)}, bf16[1024,1024]{1,0:T(8,128)(2,1)}, u32[]{:S(2)}) copy-start(bf16[1024,1024]{1,0:T(8,128)(2,1)} %param.12) | copy-start | bytes 6291460
  6.5 219.7 %reduce-scatter.2.cloned.1.call-start = ((), (), s32[]{:S(2)}) async-start(), calls=%async_computation.1 | async-start | bytes 1081344 | tf_op jit(solution)/shard_map/reduce_scatter | solution.py:63
  9.7 298.0 %all-gather.3.cloned.1.call-start = ((), (), s32[]{:S(2)}) async-start(), calls=%async_computation.2 | async-start | bytes 2162688 | tf_op jit(solution)/shard_map/all_gather | solution.py:78
  230.7 182.8 %all-gather.5.cloned.1.call-start = ((), (), s32[]{:S(2)}) async-start(), calls=%async_computation.3 | async-start | bytes 2162688 | tf_op jit(solution)/shard_map/all_gather | solution.py:91
  310.8 18.6 %collective-permute-start = (bf16[256,2048]{1,0:T(8,128)(2,1)}, bf16[256,2048]{1,0:T(8,128)(2,1)}, u32[]{:S(2)}, u32[]{:S(2)}) collective-permute-start(bf16[256,2048]{1,0:T(8,128)(2,1)} %get-tuple-element.34), channel_id=1, source_target_pairs={{0,32},{32,64},{64,96},{96,128},{128,160},{160,192},{192,224},{224... | collective-permute-start | bytes 3145736 | tf_op jit(solution)/shard_map/ppermute | solution.py:19
  317.4 14.4 %collective-permute-start.1 = (bf16[256,2048]{1,0:T(8,128)(2,1)}, bf16[256,2048]{1,0:T(8,128)(2,1)S(1)}, u32[]{:S(2)}, u32[]{:S(2)}) collective-permute-start(bf16[256,2048]{1,0:T(8,128)(2,1)} %get-tuple-element.32), channel_id=1, source_target_pairs={{32,0},{64,32},{96,64},{128,96},{160,128},{192,160},{224,192},{0,2... | collective-permute-start | bytes 3145736 | tf_op jit(solution)/shard_map/ppermute | solution.py:21
  317.4 13.4 %copy-start.1 = (bf16[512,2048]{1,0:T(8,128)(2,1)S(1)}, bf16[512,2048]{1,0:T(8,128)(2,1)}, u32[]{:S(2)}) copy-start(bf16[512,2048]{1,0:T(8,128)(2,1)} %all-gather.3.cloned.1.call-done) | copy-start | bytes 6291460
  337.2 4.5 copy-start.2
  339.6 3.5 copy-start.7
  413.4 30.8 %collective-permute-start.3 = (bf16[512,2048]{1,0:T(8,128)(2,1)}, bf16[512,2048]{1,0:T(8,128)(2,1)S(1)}, u32[]{:S(2)}, u32[]{:S(2)}) collective-permute-start(bf16[512,2048]{1,0:T(8,128)(2,1)} %all-gather.5.cloned.1.call-done), channel_id=1, source_target_pairs={{32,0},{64,32},{96,64},{128,96},{160,128},{192,160},{224,192},{0,2... | collective-permute-start | bytes 6291464 | tf_op jit(solution)/shard_map/ppermute | solution.py:21
  418.9 25.3 %collective-permute-start.2 = (bf16[512,2048]{1,0:T(8,128)(2,1)}, bf16[512,2048]{1,0:T(8,128)(2,1)S(1)}, u32[]{:S(2)}, u32[]{:S(2)}) collective-permute-start(bf16[512,2048]{1,0:T(8,128)(2,1)} %all-gather.5.cloned.1.call-done), channel_id=1, source_target_pairs={{0,32},{32,64},{64,96},{96,128},{128,160},{160,192},{192,224},{224... | collective-permute-start | bytes 6291464 | tf_op jit(solution)/shard_map/ppermute | solution.py:19
  426.9 17.3 %copy-start.5 = (bf16[512,2048]{1,0:T(8,128)(2,1)S(1)}, bf16[512,2048]{1,0:T(8,128)(2,1)}, u32[]{:S(2)}) copy-start(bf16[512,2048]{1,0:T(8,128)(2,1)} %all-gather.5.cloned.1.call-done) | copy-start | bytes 6291460
  461.4 1.3 copy-start.3
  462.7 3.9 copy-start.4
  474.3 16.3 %copy-start.6 = (bf16[768,1024]{0,1:T(8,128)(2,1)S(1)}, bf16[768,1024]{0,1:T(8,128)(2,1)}, u32[]{:S(2)}) copy-start(bf16[768,1024]{0,1:T(8,128)(2,1)} %copy.22) | copy-start | bytes 4718596
Sparse Core Ops, SparseCore 0:
  11.1 215.0 reduce-scatter.1
  230.8 76.8 all-gather.2
  343.2 70.2 all-gather.4
where the time goes:
time: 507 us
  waiting for transfers between devices  391 us (77%)
  matrix products  37.7 us (7%)
  other arithmetic  31.2 us (6%)
  local copies, waits for them, and re-layouts  20.1 us (4%)
  between operations  13.3 us (3%)
  starting transfers between devices  13.2 us (3%)
    reduce_scatter x1, waiting for transfers between devices, body(): lax.psum_scatter(jnp.dot(member, tokens, preferred_element_type=jnp.float...  216 us
    all_gather x1, waiting for transfers between devices, body(): owner_pairs = lax.all_gather(coarse_pair, 'fine', axis=0, tiled=True)  77 us
    all_gather x1, waiting for transfers between devices, body(): owner_rows = lax.all_gather(payload, 'fine', axis=0, tiled=True)  70 us
    ppermute x2, waiting for transfers between devices, padded(): lax.ppermute(head, axis, [((i + 1) % count, i) for i in range(count)])  16.5 us
    sub x1, other arithmetic, attend_heads(): expos = jnp.exp(scores - highest)  16.3 us
    ppermute x2, waiting for transfers between devices, padded(): lax.ppermute(tail, axis, [(i, (i + 1) % count) for i in range(count)])  12 us
    concatenate x1, other arithmetic, padded(): jnp.concatenate([lax.ppermute(tail, axis, [(i, (i + 1) % count) for i in...  11.2 us
  transfers between devices with their start and end apart: 7, of which 6 were waited for; matrix products, arithmetic and copies ran while one was open for 2% of the time, Pallas kernels for 0%

commit v1 on v0

--- a/solution.py
+++ b/solution.py
@@ -88,7 +88,9 @@
     state = normalize(context).astype(jnp.bfloat16)
     payload = jnp.dot(state, w_kv2, preferred_element_type=jnp.float32).astype(jnp.bfloat16)
     seg_total = seg_owned * coarse_count
-    owner_rows = lax.all_gather(payload, "fine", axis=0, tiled=True)
+    owner_rows = jnp.concatenate(
+        lax.all_to_all(jnp.stack([payload] * lax.axis_size("fine")), "fine", 0, 0), axis=0
+    )
     second_table = padded(owner_rows, (("coarse", 0),), seg_owned)
     table_base = (coarse_index - 1) * seg_owned
     proj = jnp.dot(tokens, w_qkv, preferred_element_type=jnp.float32)

time: 507 us -> 485 us (0.957)
  waiting for transfers between devices: 391 us -> 368 us
  other arithmetic: 31.2 us -> 24.9 us
    all_gather x1 -> x0, waiting for transfers between devices: 70 us -> none  [body(): owner_rows = lax.all_gather(payload, 'fine', axis=0, tiled=True)]
    all_to_all x0 -> x1, waiting for transfers between devices: none -> 46.5 us  [body(): lax.all_to_all(jnp.stack([payload] * lax.axis_size('fine')), 'fine', 0, 0)]
    concatenate x1, other arithmetic: 11.2 us -> 4.93 us  [padded(): jnp.concatenate([lax.ppermute(tail, axis, [(i, (i + 1) % count) for i in...]
    all_to_all x0 -> x1, starting transfers between devices: none -> 5.62 us  [body(): lax.all_to_all(jnp.stack([payload] * lax.axis_size('fine')), 'fine', 0, 0)]
where the time goes in v1:
time: 485 us; the launch traced here: 482 us
  waiting for transfers between devices  368 us (76%)
  matrix products  37 us (8%)
  other arithmetic  24.9 us (5%)
  local copies, waits for them, and re-layouts  21.8 us (4%)
  starting transfers between devices  17.3 us (4%)
  between operations  13.6 us (3%)
    reduce_scatter x1, waiting for transfers between devices, body(): lax.psum_scatter(jnp.dot(member, tokens, preferred_element_type=jnp.float...  216 us
    all_gather x1, waiting for transfers between devices, body(): owner_pairs = lax.all_gather(coarse_pair, 'fine', axis=0, tiled=True)  77 us
    all_to_all x1, waiting for transfers between devices, body(): lax.all_to_all(jnp.stack([payload] * lax.axis_size('fine')), 'fine', 0, 0)  46.5 us
    ppermute x2, waiting for transfers between devices, padded(): lax.ppermute(head, axis, [((i + 1) % count, i) for i in range(count)])  16.4 us
    sub x1, other arithmetic, attend_heads(): expos = jnp.exp(scores - highest)  16.2 us
    ppermute x2, waiting for transfers between devices, padded(): lax.ppermute(tail, axis, [(i, (i + 1) % count) for i in range(count)])  12 us
  transfers between devices with their start and end apart: 7, of which 6 were waited for; matrix products, arithmetic and copies ran while one was open for 2% of the time, Pallas kernels for 0%

profile of v1, /device:TPU:1, one launch (start us, length us, event | category | flops | bytes accessed | tf_op | source)
XLA Modules:
  0.0 482.3 jit_solution(3217756528330818270)
XLA Ops:
  6.5 3.1 convolution_convert_fusion.3
  9.7 0.0 reduce-scatter.2.cloned.1.call-update
  9.7 0.0 all-gather.2.cloned.1.call-start
  9.8 0.8 convert_sqrt_fusion
  10.5 215.7 %reduce-scatter.2.cloned.1.call-done = bf16[16,1024]{1,0:T(8,128)(2,1)} async-done(((bf16[512,1024]{1,0:T(8,128)(2,1)}), bf16[16,1024]{1,0:T(8,128)(2,1)}) %reduce-scatter.2.cloned.1.call-update) | async-done | bytes 32784 | tf_op jit(solution)/shard_map/reduce_scatter | solution.py:63
  226.3 3.8 convolution_convert_fusion.1
  230.0 0.6 slice.55
  230.7 0.0 all-gather.2.cloned.1.call-update
  230.7 77.0 %all-gather.2.cloned.1.call-done = bf16[512,2048]{1,0:T(8,128)(2,1)} async-done(((bf16[16,2048]{1,0:T(8,128)(2,1)}), bf16[512,2048]{1,0:T(8,128)(2,1)}) %all-gather.2.cloned.1.call-update) | async-done | bytes 2097168 | tf_op jit(solution)/shard_map/all_gather | solution.py:78
  307.7 3.1 fusion.55
  310.8 6.5 %collective-permute-start = (bf16[256,2048]{1,0:T(8,128)(2,1)}, bf16[256,2048]{1,0:T(8,128)(2,1)}, u32[]{:S(2)}, u32[]{:S(2)}) collective-permute-start(bf16[256,2048]{1,0:T(8,128)(2,1)} %get-tuple-element.34), channel_id=1, source_target_pairs={{0,32},{32,64},{64,96},{96,128},{128,160},{160,192},{192,224},{224... | collective-permute-start | bytes 3145736 | tf_op jit(solution)/shard_map/ppermute | solution.py:19
  317.4 0.1 abs_compare_fusion
  317.5 12.0 %collective-permute-done = bf16[256,2048]{1,0:T(8,128)(2,1)} collective-permute-done((bf16[256,2048]{1,0:T(8,128)(2,1)}, bf16[256,2048]{1,0:T(8,128)(2,1)}, u32[]{:S(2)}, u32[]{:S(2)}) %collective-permute-start) | collective-permute-done | bytes 1048608 | tf_op jit(solution)/shard_map/ppermute | solution.py:19
  329.5 1.3 constant_dynamic-update-slice_fusion.2
  330.8 0.1 constant_dynamic-update-slice_fusion.1
  330.9 0.9 collective-permute-done.1
  331.8 0.1 constant_dynamic-update-slice_fusion
  331.9 2.9 slice_bitcast_fusion.1
  334.8 2.4 fusion.57
  337.2 2.4 fusion.28
  339.6 2.1 multiply_reduce_fusion.1
  341.7 0.7 convolution_convert_fusion.2
  342.4 1.6 stack.2
  344.0 5.6 %all-to-all-start = ((bf16[32,16,2048]{2,1,0:T(8,128)(2,1)}), bf16[32,16,2048]{2,1,0:T(8,128)(2,1)}, u32[]{:S(2)}, u32[]{:S(2)}) async-start(bf16[32,16,2048]{2,1,0:T(8,128)(2,1)} %stack.2), calls=%async_computation.1 | async-start | bytes 4194304 | tf_op jit(solution)/shard_map/all_to_all | solution.py:92
  349.7 0.1 add.149
  349.8 0.1 add.167
  349.8 0.1 add.150
  349.9 0.1 add.152
  350.0 46.5 %all-to-all-done = bf16[32,16,2048]{2,1,0:T(8,128)(2,1)} async-done(((bf16[32,16,2048]{2,1,0:T(8,128)(2,1)}), bf16[32,16,2048]{2,1,0:T(8,128)(2,1)}, u32[]{:S(2)}, u32[]{:S(2)}) %all-to-all-start) | async-done | bytes 2097184 | tf_op jit(solution)/shard_map/all_to_all | solution.py:92
  396.5 3.3 collective-permute-start.3
  399.9 1.8 collective-permute-start.2
  401.7 0.1 broadcast_compare_fusion
  401.8 0.1 concatenate.20
  402.0 6.5 %convolution_convert_fusion = bf16[512,3072]{1,0:T(8,128)(2,1)S(1)} fusion(bf16[512,1024]{1,0:T(8,128)(2,1)} %param.8, bf16[1024,3072]{1,0:T(8,128)(2,1)} %param.9), kind=kOutput, calls=%fused_computation.12 | convolution fusion | flops 3222798336 | bytes 10485760 | tf_op jit(solution)/shard_map/dot_general | solution.py:96
  408.5 1.8 slice_bitcast_fusion.2
  410.3 15.5 %collective-permute-done.3 = bf16[512,2048]{1,0:T(8,128)(2,1)S(1)} collective-permute-done((bf16[512,2048]{1,0:T(8,128)(2,1)}, bf16[512,2048]{1,0:T(8,128)(2,1)S(1)}, u32[]{:S(2)}, u32[]{:S(2)}) %collective-permute-start.3) | collective-permute-done | bytes 2097184 | tf_op jit(solution)/shard_map/ppermute | solution.py:21
  425.9 4.9 %pad_maximum_fusion = bf16[1536,2048]{1,0:T(8,128)(2,1)} fusion(bf16[512,2048]{1,0:T(8,128)(2,1)S(1)} %collective-permute-done.3, bf16[512,2048]{1,0:T(8,128)(2,1)} %bitcast.2, bf16[512,2048]{1,0:T(8,128)(2,1)S(1)} %collective-permute-done.2), kind=kLoop, calls=%fused_computation.7 | loop fusion | flops 18874368 | bytes 12582912 | tf_op jit(solution)/shard_map/concatenate | solution.py:17
  430.8 6.0 %gather_fusion = bf16[256,2048]{1,0:T(8,128)(2,1)S(1)} fusion(bf16[1536,2048]{1,0:T(8,128)(2,1)} %pad_maximum_fusion, s32[1024]{0:T(1024)S(1)} %pad_clamp_fusion), kind=kCustom, calls=%fused_computation | custom fusion | bytes 2098176 | tf_op jit(solution)/shard_map/while/body/eval_jaxpr/jit(_take)/gather | solution.py:119
  436.8 0.2 broadcast_select_fusion
  436.9 0.9 fusion.56
  437.8 0.3 copy-done.3
  438.1 1.3 pad_maximum_fusion.1
  439.4 2.6 copy.22
  442.0 7.7 %fusion.13 = f32[8,512,768]{2,1,0:T(8,128)} fusion(bf16[64,8,8,128]{3,2,1,0:T(8,128)(2,1)S(1)} %copy-done.4, bf16[256,1024]{1,0:T(8,128)(2,1)} %get-tuple-element.36, bf16[512,1024]{1,0:T(8,128)(2,1)} %get-tuple-element.22), kind=kOutput, calls=%fused_computation.25 | convolution fusion | flops 808452096 | bytes 15204352 | tf_op jit(solution)/shard_map/while/body/eval_jaxpr/qhd,khd->hqk/dot_general | solution.py:34
  449.7 16.2 %fusion.58 = (f32[8,512]{1,0:T(8,128)S(1)}, f32[8,512,768]{2,1,0:T(8,128)}) fusion(f32[8,512,768]{2,1,0:T(8,128)} %fusion.13, pred[512,768]{1,0:T(8,128)(4,1)S(1)} %concatenate.20), kind=kOutput, calls=%fused_computation.102 | output fusion | flops 18875136 | bytes 25575424 | tf_op jit(solution)/shard_map/while/body/eval_jaxpr/sub | solution.py:38
  466.0 6.9 %fusion.16 = bf16[8,128,512]{2,1,0:T(8,128)(2,1)S(1)} fusion(bf16[768,8,128]{0,2,1:T(8,128)(2,1)S(1)} %bitcast.74, f32[8,512,768]{2,1,0:T(8,128)} %get-tuple-element.43, f32[8,512]{1,0:T(8,128)S(1)} %get-tuple-element.42), kind=kOutput, calls=%fused_computation.31 | convolution fusion | flops 812122112 | bytes 15220736 | tf_op jit(solution)/shard_map/while/body/eval_jaxpr/hqk,khd->qhd/dot_general | solution.py:40
  472.9 1.4 multiply_reduce_fusion
  474.3 1.2 multiply_convert_fusion
  (28 shorter events, 0.1 us)
Async XLA Ops:
  6.5 466.3 %copy-start = (bf16[1024,1024]{1,0:T(8,128)(2,1)S(1)}, bf16[1024,1024]{1,0:T(8,128)(2,1)}, u32[]{:S(2)}) copy-start(bf16[1024,1024]{1,0:T(8,128)(2,1)} %param.12) | copy-start | bytes 6291460
  6.5 219.7 %reduce-scatter.2.cloned.1.call-start = ((), (), s32[]{:S(2)}) async-start(), calls=%async_computation.2 | async-start | bytes 1081344 | tf_op jit(solution)/shard_map/reduce_scatter | solution.py:63
  9.7 298.0 %all-gather.2.cloned.1.call-start = ((), (), s32[]{:S(2)}) async-start(), calls=%async_computation.3 | async-start | bytes 2162688 | tf_op jit(solution)/shard_map/all_gather | solution.py:78
  310.8 18.6 %collective-permute-start = (bf16[256,2048]{1,0:T(8,128)(2,1)}, bf16[256,2048]{1,0:T(8,128)(2,1)}, u32[]{:S(2)}, u32[]{:S(2)}) collective-permute-start(bf16[256,2048]{1,0:T(8,128)(2,1)} %get-tuple-element.34), channel_id=1, source_target_pairs={{0,32},{32,64},{64,96},{96,128},{128,160},{160,192},{192,224},{224... | collective-permute-start | bytes 3145736 | tf_op jit(solution)/shard_map/ppermute | solution.py:19
  317.4 14.4 %collective-permute-start.1 = (bf16[256,2048]{1,0:T(8,128)(2,1)}, bf16[256,2048]{1,0:T(8,128)(2,1)S(1)}, u32[]{:S(2)}, u32[]{:S(2)}) collective-permute-start(bf16[256,2048]{1,0:T(8,128)(2,1)} %get-tuple-element.32), channel_id=1, source_target_pairs={{32,0},{64,32},{96,64},{128,96},{160,128},{192,160},{224,192},{0,2... | collective-permute-start | bytes 3145736 | tf_op jit(solution)/shard_map/ppermute | solution.py:21
  317.4 13.4 %copy-start.1 = (bf16[512,2048]{1,0:T(8,128)(2,1)S(1)}, bf16[512,2048]{1,0:T(8,128)(2,1)}, u32[]{:S(2)}) copy-start(bf16[512,2048]{1,0:T(8,128)(2,1)} %all-gather.2.cloned.1.call-done) | copy-start | bytes 6291460
  337.2 4.5 copy-start.2
  342.4 7.2 %copy-start.6 = (s32[2,8]{1,0:T(2,128)S(1)}, s32[2,8]{1,0:T(2,128)}, u32[]{:S(2)}) copy-start(s32[2,8]{1,0:T(2,128)} %param.15) | copy-start | bytes 196
  344.0 52.5 %all-to-all-start = ((bf16[32,16,2048]{2,1,0:T(8,128)(2,1)}), bf16[32,16,2048]{2,1,0:T(8,128)(2,1)}, u32[]{:S(2)}, u32[]{:S(2)}) async-start(bf16[32,16,2048]{2,1,0:T(8,128)(2,1)} %stack.2), calls=%async_computation.1 | async-start | bytes 4194304 | tf_op jit(solution)/shard_map/all_to_all | solution.py:92
  396.5 29.3 %collective-permute-start.3 = (bf16[512,2048]{1,0:T(8,128)(2,1)}, bf16[512,2048]{1,0:T(8,128)(2,1)S(1)}, u32[]{:S(2)}, u32[]{:S(2)}) collective-permute-start(bf16[512,2048]{1,0:T(8,128)(2,1)} %bitcast.2), channel_id=1, source_target_pairs={{32,0},{64,32},{96,64},{128,96},{160,128},{192,160},{224,192},{0,2... | collective-permute-start | bytes 6291464 | tf_op jit(solution)/shard_map/ppermute | solution.py:21
  399.9 26.0 %collective-permute-start.2 = (bf16[512,2048]{1,0:T(8,128)(2,1)}, bf16[512,2048]{1,0:T(8,128)(2,1)S(1)}, u32[]{:S(2)}, u32[]{:S(2)}) collective-permute-start(bf16[512,2048]{1,0:T(8,128)(2,1)} %bitcast.2), channel_id=1, source_target_pairs={{0,32},{32,64},{64,96},{96,128},{128,160},{160,192},{192,224},{224... | collective-permute-start | bytes 6291464 | tf_op jit(solution)/shard_map/ppermute | solution.py:19
  436.8 1.3 copy-start.3
  438.1 3.9 copy-start.4
  449.7 16.2 %copy-start.5 = (bf16[768,1024]{0,1:T(8,128)(2,1)S(1)}, bf16[768,1024]{0,1:T(8,128)(2,1)}, u32[]{:S(2)}) copy-start(bf16[768,1024]{0,1:T(8,128)(2,1)} %copy.22) | copy-start | bytes 4718596
Sparse Core Ops, SparseCore 0:
  11.1 215.0 reduce-scatter.1
  230.8 76.8 all-gather.1
